TPU v7x, 32 devices: a whole 2x2x4 slice. The times are simulated.
32 devices in a mesh: ctx: 8 (over y, x, core), exp: 4 (over z).
Axes of the slice: x: 2, y: 2, z: 4, core: 2. Of those that a mesh axis runs over, the one named last changes fastest.
Arguments:
- tokens: bfloat16 [4096, 2048], P(('ctx', 'exp')), may hold values from -6 to 6
- cotangent: bfloat16 [4096, 2048], P(('ctx', 'exp')), may hold values from -6 to 6
- expert_ids: int32 [4096, 1], P(('ctx', 'exp')), may hold values from 0 to 3; in each aligned block of 128 rows (0 to 127, 128 to 255, ...) at most 48 rows name the same one
- route_weights: float32 [4096, 1], P(('ctx', 'exp')), may hold values from 0.1 to 1
- w_gate: bfloat16 [4, 2048, 768], P('exp', 'ctx'), may hold values from -0.125 to 0.125
- w_up: bfloat16 [4, 2048, 768], P('exp', 'ctx'), may hold values from -0.125 to 0.125
- w_down: bfloat16 [4, 768, 2048], P('exp', None, 'ctx'), may hold values from -0.21875 to 0.21875
Outputs:
- token_grads: bfloat16 [4096, 2048], P(('ctx', 'exp'))
- route_grads: float32 [4096, 1], P(('ctx', 'exp'))
- gate_grads: bfloat16 [4, 2048, 768], P('exp', 'ctx')
- up_grads: bfloat16 [4, 2048, 768], P('exp', 'ctx')
- down_grads: bfloat16 [4, 768, 2048], P('exp', None, 'ctx')
Inputs may be any that keep to these rules, and one draw needn't show every extreme that they name: `expert_ids`: among the 128 routes of one device's tokens no expert is named more than 48 times, a bound that some block reaches; the routes of one token name different experts.
All inputs are finite; a program needn't handle non-finite values.
Results may differ from a plain program's by a relative error of at most 0.018.
Values may be sent and summed in bfloat16 or wider, within the bound.
A program may use at most 64 MiB of HBM per device.

v0:
```python
import jax
import jax.numpy as jnp
from jax import lax
from jax.sharding import PartitionSpec as P


def slot_table(route_ids, expert_count, capacity):
    labels = jnp.arange(expert_count, dtype=jnp.int32)
    onehot = (route_ids[..., :, None] == labels).astype(jnp.int32)
    position = jnp.sum((jnp.cumsum(onehot, axis=-2) - 1) * onehot, axis=-1)
    target = route_ids * capacity + position
    places = jnp.arange(expert_count * capacity, dtype=jnp.int32)
    return (target[..., None, :] == places[:, None]).astype(jnp.bfloat16)


def forward_hidden(totals, units):
    gate_pre = totals[:, :units]
    up_pre = totals[:, units:]
    gate_sig = jax.nn.sigmoid(gate_pre)
    return (gate_pre * gate_sig * up_pre).astype(jnp.bfloat16)


def backward_grads(totals, back_sum, units):
    gate_pre = totals[:, :units]
    up_pre = totals[:, units:]
    gate_sig = jax.nn.sigmoid(gate_pre)
    d_up = (back_sum * gate_pre * gate_sig).astype(jnp.bfloat16)
    d_gate = (back_sum * up_pre * gate_sig * (1.0 + gate_pre * (1.0 - gate_sig))).astype(
        jnp.bfloat16
    )
    return jnp.concatenate([d_gate, d_up], axis=1)


def body(tokens, cotangent, expert_ids, route_weights, w_gate, w_up, w_down):
    ctx_size = lax.axis_size("ctx")
    exp_size = lax.axis_size("exp")
    tok_count, model_width = tokens.shape
    route_count = expert_ids.shape[1]
    slot_count = tok_count * route_count
    expert_count = w_gate.shape[0] * exp_size
    capacity = max(2, (3 * slot_count + 2 * expert_count - 1) // (2 * expert_count))
    col_count = model_width // ctx_size
    units = w_gate.shape[2]
    row_count = ctx_size * exp_size * capacity
    own_rows = row_count // ctx_size
    all_ids = lax.all_gather(expert_ids, "ctx", axis=0, tiled=True)
    tables = slot_table(all_ids.reshape(ctx_size, slot_count), expert_count, capacity)
    token_slots = jnp.repeat(tokens, route_count, axis=0)
    scaled = (
        route_weights * jnp.repeat(cotangent, route_count, axis=0).astype(jnp.float32)
    ).astype(jnp.bfloat16)
    own_table = lax.dynamic_index_in_dim(tables, lax.axis_index("ctx"), 0, keepdims=False)
    send_x = jnp.dot(own_table, token_slots, preferred_element_type=jnp.float32).astype(
        jnp.bfloat16
    )
    send_y = jnp.dot(own_table, scaled, preferred_element_type=jnp.float32).astype(jnp.bfloat16)
    send_x = send_x.reshape(expert_count, capacity, model_width)
    send_y = send_y.reshape(expert_count, capacity, model_width)
    group_x, group_y = (
        lax.all_to_all(send_x, "exp", split_axis=0, concat_axis=0, tiled=True),
        lax.all_to_all(send_y, "exp", split_axis=0, concat_axis=0, tiled=True),
    )
    slot_x, slot_y = (
        lax.all_to_all(group_x, "ctx", split_axis=2, concat_axis=0, tiled=True),
        lax.all_to_all(group_y, "ctx", split_axis=2, concat_axis=0, tiled=True),
    )
    slot_x = slot_x.reshape(row_count, col_count)
    slot_y = slot_y.reshape(row_count, col_count)
    gate_weight = w_gate[0]
    up_weight = w_up[0]
    down_weight = w_down[0]
    both_weights = jnp.concatenate([gate_weight, up_weight], axis=1)

    def fold_grad(segment):
        gate_acc = lax.dot_general(
            slot_x, segment[:, :units], (((0,), (0,)), ((), ())), preferred_element_type=jnp.float32
        )
        up_acc = lax.dot_general(
            slot_x, segment[:, units:], (((0,), (0,)), ((), ())), preferred_element_type=jnp.float32
        )
        grad_rows = lax.dot_general(
            segment, both_weights, (((1,), (1,)), ((), ())), preferred_element_type=jnp.float32
        )
        return (gate_acc, up_acc, grad_rows)

    row_x, row_y = (
        lax.all_to_all(slot_x, "ctx", split_axis=0, concat_axis=1, tiled=True),
        lax.all_to_all(slot_y, "ctx", split_axis=0, concat_axis=1, tiled=True),
    )
    full_gate, full_up, full_down = (
        lax.all_gather(gate_weight, "ctx", axis=0, tiled=True),
        lax.all_gather(up_weight, "ctx", axis=0, tiled=True),
        lax.all_gather(down_weight, "ctx", axis=1, tiled=True),
    )
    full_both = jnp.concatenate([full_gate, full_up], axis=1).reshape(
        ctx_size, col_count, 2 * units
    )
    gate_blocks = jnp.einsum(
        "rcd,cdf->crf",
        row_x.reshape(own_rows, ctx_size, col_count),
        full_both,
        preferred_element_type=jnp.float32,
    ).astype(jnp.bfloat16)
    totals_own = jnp.sum(gate_blocks.astype(jnp.float32), axis=0)
    hidden_own = forward_hidden(totals_own, units)
    back_blocks = jnp.einsum(
        "rcd,fcd->crf",
        row_y.reshape(own_rows, ctx_size, col_count),
        full_down.reshape(units, ctx_size, col_count),
        preferred_element_type=jnp.float32,
    ).astype(jnp.bfloat16)
    back_own = jnp.sum(back_blocks.astype(jnp.float32), axis=0)
    grads_own = backward_grads(totals_own, back_own, units)
    segment = (
        lax.all_gather(hidden_own, "ctx", axis=0, tiled=True),
        lax.all_gather(grads_own, "ctx", axis=0, tiled=True),
    )
    fold_segment = segment[0]
    outputs = jnp.dot(fold_segment, down_weight, preferred_element_type=jnp.float32)
    inner_rows = jnp.sum(slot_y.astype(jnp.float32) * outputs, axis=1)
    inner_all = inner_rows
    down_acc = lax.dot_general(
        fold_segment, slot_y, (((0,), (0,)), ((), ())), preferred_element_type=jnp.float32
    )
    down_state = (down_acc, inner_all)
    grad_state = fold_grad(segment[1])
    down_acc = down_state[0]
    inner_all = down_state[1]
    gate_acc = grad_state[0]
    up_acc = grad_state[1]
    back_rows = grad_state[2]
    back_slots = back_rows.astype(jnp.bfloat16).reshape(ctx_size, exp_size, capacity, col_count)
    inner_slots = inner_all.reshape(ctx_size, exp_size, capacity)
    home_back = lax.all_to_all(back_slots, "exp", split_axis=1, concat_axis=1, tiled=True)
    home_inner = lax.all_to_all(inner_slots, "exp", split_axis=1, concat_axis=1, tiled=True)
    merged = jnp.einsum(
        "cks,ckd->csd",
        tables,
        home_back.reshape(ctx_size, expert_count * capacity, col_count),
        preferred_element_type=jnp.float32,
    )
    merged = jnp.sum(merged.reshape(ctx_size, tok_count, route_count, col_count), axis=2).astype(
        jnp.bfloat16
    )
    grads_home = lax.all_to_all(merged, "ctx", split_axis=0, concat_axis=2, tiled=True)
    token_grads = grads_home.reshape(tok_count, model_width)
    inner_home = jnp.einsum(
        "cks,ck->cs",
        tables.astype(jnp.float32),
        home_inner.reshape(ctx_size, expert_count * capacity),
        precision=lax.Precision.HIGHEST,
    )
    route_sums = lax.psum_scatter(inner_home, "ctx", scatter_dimension=0, tiled=True).reshape(
        tok_count, route_count
    )
    route_grads = route_sums / route_weights
    gate_grads = gate_acc.astype(jnp.bfloat16)[None]
    up_grads = up_acc.astype(jnp.bfloat16)[None]
    down_grads = down_acc.astype(jnp.bfloat16)[None]
    return (token_grads, route_grads, gate_grads, up_grads, down_grads)


def solution(mesh):
    return jax.shard_map(
        body,
        mesh=mesh,
        in_specs=(
            P(("ctx", "exp"), None),
            P(("ctx", "exp"), None),
            P(("ctx", "exp"), None),
            P(("ctx", "exp"), None),
            P("exp", "ctx", None),
            P("exp", "ctx", None),
            P("exp", None, "ctx"),
        ),
        out_specs=(
            P(("ctx", "exp"), None),
            P(("ctx", "exp"), None),
            P("exp", "ctx", None),
            P("exp", "ctx", None),
            P("exp", None, "ctx"),
        ),
        check_vma=False,
    )
```

profile of v0, /device:TPU:0, one launch (start us, length us, event | category | flops | bytes accessed | tf_op | source)
XLA Modules:
  0.0 269.7 jit_solution(1433237262053152039)
XLA Ops:
  10.7 10.3 %all_gather.18 = s32[1024,1]{0,1:T(1,128)S(1)} all-gather(s32[128,1]{0,1:T(1,128)} %param.9), channel_id=1, replica_groups=mesh['ctx'=8,'exp'=4] {'ctx'}, dimensions={0}, use_global_device_ids=true | all-gather | bytes 4608 | tf_op jit(solution)/shard_map/all_gather | solution.py:46
  26.2 4.9 %all-to-all-start = ((bf16[4,48,2048]{2,1,0:T(8,128)(2,1)}), bf16[4,48,2048]{2,1,0:T(8,128)(2,1)S(1)}, u32[]{:S(2)}, u32[]{:S(2)}) async-start(bf16[4,48,2048]{2,1,0:T(8,128)(2,1)} %bitcast.3), calls=%async_computation | async-start | bytes 1572864 | tf_op jit(solution)/shard_map/all_to_all | solution.py:61
  32.4 19.3 %all-to-all-done = bf16[4,48,2048]{2,1,0:T(8,128)(2,1)S(1)} async-done(((bf16[4,48,2048]{2,1,0:T(8,128)(2,1)}), bf16[4,48,2048]{2,1,0:T(8,128)(2,1)S(1)}, u32[]{:S(2)}, u32[]{:S(2)}) %all-to-all-start) | async-done | bytes 786464 | tf_op jit(solution)/shard_map/all_to_all | solution.py:61
  52.6 3.5 %all-to-all-start.3 = ((bf16[4,48,2048]{2,1,0:T(8,128)(2,1)}), bf16[4,48,2048]{2,1,0:T(8,128)(2,1)S(1)}, u32[]{:S(2)}, u32[]{:S(2)}) async-start(bf16[4,48,2048]{2,1,0:T(8,128)(2,1)} %bitcast.10), calls=%async_computation.3 | async-start | bytes 1572864 | tf_op jit(solution)/shard_map/all_to_all | solution.py:60
  59.0 4.0 %reshape.98 = bf16[8,2,24576]{2,1,0:T(2,128)(2,1)} reshape(bf16[2048,4,48]{2,1,0:T(4,128)(2,1)S(1)} %bitcast.76) | data formatting | bytes 1572864
  63.0 12.9 %all-to-all-done.3 = bf16[4,48,2048]{2,1,0:T(8,128)(2,1)S(1)} async-done(((bf16[4,48,2048]{2,1,0:T(8,128)(2,1)}), bf16[4,48,2048]{2,1,0:T(8,128)(2,1)S(1)}, u32[]{:S(2)}, u32[]{:S(2)}) %all-to-all-start.3) | async-done | bytes 786464 | tf_op jit(solution)/shard_map/all_to_all | solution.py:60
  75.8 4.2 %all-to-all-start.1 = ((bf16[8,2,24576]{2,1,0:T(2,128)(2,1)}), bf16[8,2,24576]{2,1,0:T(2,128)(2,1)}, u32[]{:S(2)}, u32[]{:S(2)}) async-start(bf16[8,2,24576]{2,1,0:T(2,128)(2,1)} %reshape.98), calls=%async_computation.1 | async-start | bytes 1572864 | tf_op jit(solution)/shard_map/all_to_all | solution.py:65
  81.5 4.0 %reshape.100 = bf16[8,2,24576]{2,1,0:T(2,128)(2,1)} reshape(bf16[2048,4,48]{2,1,0:T(4,128)(2,1)S(1)} %bitcast.77) | data formatting | bytes 1572864
  85.4 7.3 %all-to-all-done.1 = bf16[8,2,24576]{2,1,0:T(2,128)(2,1)} async-done(((bf16[8,2,24576]{2,1,0:T(2,128)(2,1)}), bf16[8,2,24576]{2,1,0:T(2,128)(2,1)}, u32[]{:S(2)}, u32[]{:S(2)}) %all-to-all-start.1) | async-done | bytes 786464 | tf_op jit(solution)/shard_map/all_to_all | solution.py:65
  92.7 3.5 %all-to-all-start.4 = ((bf16[8,2,24576]{2,1,0:T(2,128)(2,1)}), bf16[8,2,24576]{2,1,0:T(2,128)(2,1)S(1)}, u32[]{:S(2)}, u32[]{:S(2)}) async-start(bf16[8,2,24576]{2,1,0:T(2,128)(2,1)} %reshape.100), calls=%async_computation.4 | async-start | bytes 1572864 | tf_op jit(solution)/shard_map/all_to_all | solution.py:64
  96.3 5.7 %reshape.99 = bf16[2048,4,48]{2,1,0:T(4,128)(2,1)S(1)} reshape(bf16[8,2,24576]{2,1,0:T(2,128)(2,1)} %all-to-all-done.1) | data formatting | bytes 1572864
  104.1 8.9 %all-to-all-done.4 = bf16[8,2,24576]{2,1,0:T(2,128)(2,1)S(1)} async-done(((bf16[8,2,24576]{2,1,0:T(2,128)(2,1)}), bf16[8,2,24576]{2,1,0:T(2,128)(2,1)S(1)}, u32[]{:S(2)}, u32[]{:S(2)}) %all-to-all-start.4) | async-done | bytes 786464 | tf_op jit(solution)/shard_map/all_to_all | solution.py:64
  113.0 4.4 %all-to-all-start.2 = ((bf16[8,192,256]{2,1,0:T(8,128)(2,1)}), bf16[8,192,256]{2,1,0:T(8,128)(2,1)}, u32[]{:S(2)}, u32[]{:S(2)}) async-start(bf16[8,192,256]{2,1,0:T(8,128)(2,1)} %bitcast.7), calls=%async_computation.2 | async-start | bytes 1572864 | tf_op jit(solution)/shard_map/all_to_all | solution.py:88
  121.7 8.2 %all-to-all-done.2 = bf16[8,192,256]{2,1,0:T(8,128)(2,1)} async-done(((bf16[8,192,256]{2,1,0:T(8,128)(2,1)}), bf16[8,192,256]{2,1,0:T(8,128)(2,1)}, u32[]{:S(2)}, u32[]{:S(2)}) %all-to-all-start.2) | async-done | bytes 786464 | tf_op jit(solution)/shard_map/all_to_all | solution.py:88
  129.9 3.5 %all-to-all-start.5 = ((bf16[8,192,256]{2,1,0:T(8,128)(2,1)}), bf16[8,192,256]{2,1,0:T(8,128)(2,1)S(1)}, u32[]{:S(2)}, u32[]{:S(2)}) async-start(bf16[8,192,256]{2,1,0:T(8,128)(2,1)} %bitcast.13), calls=%async_computation.5 | async-start | bytes 1572864 | tf_op jit(solution)/shard_map/all_to_all | solution.py:87
  136.5 6.0 %pad_maximum_fusion = bf16[2048,1536]{1,0:T(8,128)(2,1)} fusion(bf16[2048,768]{1,0:T(8,128)(2,1)} %bitcast.83, bf16[2048,768]{1,0:T(8,128)(2,1)} %bitcast.82), kind=kLoop, calls=%fused_computation.1 | loop fusion | flops 12582912 | bytes 12582912 | tf_op jit(solution)/shard_map/concatenate | solution.py:95
  145.9 4.2 %convert_reduce_fusion = f32[192,1536]{1,0:T(8,128)S(1)} fusion(bf16[8,256,1536]{2,1,0:T(8,128)(2,1)} %bitcast.80, bf16[8,192,256]{2,1,0:T(8,128)(2,1)S(1)} %all-to-all-done.5), kind=kOutput, calls=%fused_computation | convolution fusion | flops 1214742528 | bytes 8257536 | tf_op jit(solution)/shard_map/rcd,cdf->crf/dot_general | solution.py:98
  153.7 23.1 %all-gather.11.cloned.1.call-done = bf16[1536,768]{1,0:T(8,128)(2,1)} async-done(((bf16[192,768]{1,0:T(8,128)(2,1)}), bf16[1536,768]{1,0:T(8,128)(2,1)}) %all-gather.11.cloned.1.call-update) | async-done | bytes 2359312 | tf_op jit(solution)/shard_map/all_gather | solution.py:115
  180.1 4.6 %all-to-all-start.8 = ((f32[4,1,384]{2,1,0:T(1,128)}), f32[4,1,384]{2,1,0:T(1,128)S(1)}, u32[]{:S(2)}, u32[]{:S(2)}) async-start(f32[4,1,384]{2,1,0:T(1,128)} %reshape.102), calls=%async_computation.8 | async-start | bytes 12288 | tf_op jit(solution)/shard_map/all_to_all | solution.py:135
  184.7 32.8 %all-gather.9.cloned.1.call-done = bf16[1536,1536]{1,0:T(8,128)(2,1)} async-done(((bf16[192,1536]{1,0:T(8,128)(2,1)}), bf16[1536,1536]{1,0:T(8,128)(2,1)}) %all-gather.9.cloned.1.call-update) | async-done | bytes 4718608 | tf_op jit(solution)/shard_map/all_gather | solution.py:116
  217.5 3.8 %convolution_convert_fusion = bf16[1536,256]{1,0:T(8,128)(2,1)S(1)} fusion(bf16[1536,1536]{1,0:T(8,128)(2,1)} %all-gather.9.cloned.1.call-done, bf16[256,768]{1,0:T(8,128)(2,1)S(1)} %bitcast.88, bf16[256,768]{1,0:T(8,128)(2,1)S(1)} %bitcast.87), kind=kOutput, calls=%fused_computation.4 | convolution fusion | flops 1209925632 | bytes 6291456 | tf_op jit(solution)/shard_map/dot_general | solution.py:81
  222.2 4.6 %all-to-all-start.6 = ((bf16[8,4,48,256]{3,2,0,1:T(8,128)(2,1)}), bf16[8,4,48,256]{3,2,0,1:T(8,128)(2,1)S(1)}, u32[]{:S(2)}, u32[]{:S(2)}) async-start(bf16[8,4,48,256]{3,2,0,1:T(8,128)(2,1)} %copy.91), calls=%async_computation.6 | async-start | bytes 1572864 | tf_op jit(solution)/shard_map/all_to_all | solution.py:134
  232.6 13.1 %all-reduce = f32[8,128]{1,0:T(8,128)S(1)} all-reduce(f32[8,128]{1,0:T(8,128)S(1)} %bitcast.93), channel_id=5, replica_groups=mesh['ctx'=8,'exp'=4] {'ctx'}, use_global_device_ids=true, to_apply=%region_5.6.clone | all-reduce | flops 1024 | bytes 8192
  248.7 3.5 %all-to-all-start.7 = ((bf16[8,128,256]{2,1,0:T(8,128)(2,1)}), bf16[8,128,256]{2,1,0:T(8,128)(2,1)S(1)}, u32[]{:S(2)}, u32[]{:S(2)}) async-start(bf16[8,128,256]{2,1,0:T(8,128)(2,1)} %convolution_convert_fusion.3), calls=%async_computation.7 | async-start | bytes 1048576 | tf_op jit(solution)/shard_map/all_to_all | solution.py:145
  (68 shorter events, 55.4 us)
Async XLA Ops:
  7.2 23.9 %copy-start = (bf16[128,2048]{1,0:T(8,128)(2,1)S(1)}, bf16[128,2048]{1,0:T(8,128)(2,1)}, u32[]{:S(2)}) copy-start(bf16[128,2048]{1,0:T(8,128)(2,1)} %param.7) | copy-start | bytes 1572868
  7.2 126.3 %all-gather.13.cloned.1.call-start = ((), (), s32[]{:S(2)}) async-start(), calls=%async_computation.11 | async-start | bytes 3538944 | tf_op jit(solution)/shard_map/all_gather | solution.py:93
  9.2 127.3 %all-gather.15.cloned.1.call-start = ((), (), s32[]{:S(2)}) async-start(), calls=%async_computation.12 | async-start | bytes 3538944 | tf_op jit(solution)/shard_map/all_gather | solution.py:91
  10.0 126.5 %all-gather.17.cloned.1.call-start = ((), (), s32[]{:S(2)}) async-start(), calls=%async_computation.13 | async-start | bytes 3538944 | tf_op jit(solution)/shard_map/all_gather | solution.py:92
  26.2 25.5 %all-to-all-start = ((bf16[4,48,2048]{2,1,0:T(8,128)(2,1)}), bf16[4,48,2048]{2,1,0:T(8,128)(2,1)S(1)}, u32[]{:S(2)}, u32[]{:S(2)}) async-start(bf16[4,48,2048]{2,1,0:T(8,128)(2,1)} %bitcast.3), calls=%async_computation | async-start | bytes 1572864 | tf_op jit(solution)/shard_map/all_to_all | solution.py:61
  51.7 0.9 copy-start.1
  52.6 23.2 %all-to-all-start.3 = ((bf16[4,48,2048]{2,1,0:T(8,128)(2,1)}), bf16[4,48,2048]{2,1,0:T(8,128)(2,1)S(1)}, u32[]{:S(2)}, u32[]{:S(2)}) async-start(bf16[4,48,2048]{2,1,0:T(8,128)(2,1)} %bitcast.10), calls=%async_computation.3 | async-start | bytes 1572864 | tf_op jit(solution)/shard_map/all_to_all | solution.py:60
  75.8 16.9 %all-to-all-start.1 = ((bf16[8,2,24576]{2,1,0:T(2,128)(2,1)}), bf16[8,2,24576]{2,1,0:T(2,128)(2,1)}, u32[]{:S(2)}, u32[]{:S(2)}) async-start(bf16[8,2,24576]{2,1,0:T(2,128)(2,1)} %reshape.98), calls=%async_computation.1 | async-start | bytes 1572864 | tf_op jit(solution)/shard_map/all_to_all | solution.py:65
  92.7 20.3 %all-to-all-start.4 = ((bf16[8,2,24576]{2,1,0:T(2,128)(2,1)}), bf16[8,2,24576]{2,1,0:T(2,128)(2,1)S(1)}, u32[]{:S(2)}, u32[]{:S(2)}) async-start(bf16[8,2,24576]{2,1,0:T(2,128)(2,1)} %reshape.100), calls=%async_computation.4 | async-start | bytes 1572864 | tf_op jit(solution)/shard_map/all_to_all | solution.py:64
  113.0 16.8 %all-to-all-start.2 = ((bf16[8,192,256]{2,1,0:T(8,128)(2,1)}), bf16[8,192,256]{2,1,0:T(8,128)(2,1)}, u32[]{:S(2)}, u32[]{:S(2)}) async-start(bf16[8,192,256]{2,1,0:T(8,128)(2,1)} %bitcast.7), calls=%async_computation.2 | async-start | bytes 1572864 | tf_op jit(solution)/shard_map/all_to_all | solution.py:88
  129.9 16.1 %all-to-all-start.5 = ((bf16[8,192,256]{2,1,0:T(8,128)(2,1)}), bf16[8,192,256]{2,1,0:T(8,128)(2,1)S(1)}, u32[]{:S(2)}, u32[]{:S(2)}) async-start(bf16[8,192,256]{2,1,0:T(8,128)(2,1)} %bitcast.13), calls=%async_computation.5 | async-start | bytes 1572864 | tf_op jit(solution)/shard_map/all_to_all | solution.py:87
  133.4 43.4 %all-gather.11.cloned.1.call-start = ((), (), s32[]{:S(2)}) async-start(), calls=%async_computation.10 | async-start | bytes 2654208 | tf_op jit(solution)/shard_map/all_gather | solution.py:115
  150.2 26.6 %copy-start.2 = (bf16[1,768,256]{2,1,0:T(8,128)(2,1)S(1)}, bf16[1,768,256]{2,1,0:T(8,128)(2,1)}, u32[]{:S(2)}) copy-start(bf16[1,768,256]{2,1,0:T(8,128)(2,1)} %param.13) | copy-start | bytes 1179652
  151.3 66.2 %all-gather.9.cloned.1.call-start = ((), (), s32[]{:S(2)}) async-start(), calls=%async_computation.9 | async-start | bytes 5308416 | tf_op jit(solution)/shard_map/all_gather | solution.py:116
  152.2 65.3 %copy-start.3 = (bf16[1,256,768]{2,1,0:T(8,128)(2,1)S(1)}, bf16[1,256,768]{2,1,0:T(8,128)(2,1)}, u32[]{:S(2)}) copy-start(bf16[1,256,768]{2,1,0:T(8,128)(2,1)} %param.11) | copy-start | bytes 1179652
  152.2 65.3 %copy-start.4 = (bf16[1,256,768]{2,1,0:T(8,128)(2,1)S(1)}, bf16[1,256,768]{2,1,0:T(8,128)(2,1)}, u32[]{:S(2)}) copy-start(bf16[1,256,768]{2,1,0:T(8,128)(2,1)} %param.12) | copy-start | bytes 1179652
  180.1 42.1 %all-to-all-start.8 = ((f32[4,1,384]{2,1,0:T(1,128)}), f32[4,1,384]{2,1,0:T(1,128)S(1)}, u32[]{:S(2)}, u32[]{:S(2)}) async-start(f32[4,1,384]{2,1,0:T(1,128)} %reshape.102), calls=%async_computation.8 | async-start | bytes 12288 | tf_op jit(solution)/shard_map/all_to_all | solution.py:135
  221.2 5.6 %copy-start.6 = (u32[32]{0:T(128)S(1)}, u32[32]{0:T(128)}, u32[]{:S(2)}) copy-start(u32[32]{0:T(128)} %constant.31) | copy-start | bytes 388
  222.2 25.1 %all-to-all-start.6 = ((bf16[8,4,48,256]{3,2,0,1:T(8,128)(2,1)}), bf16[8,4,48,256]{3,2,0,1:T(8,128)(2,1)S(1)}, u32[]{:S(2)}, u32[]{:S(2)}) async-start(bf16[8,4,48,256]{3,2,0,1:T(8,128)(2,1)} %copy.91), calls=%async_computation.6 | async-start | bytes 1572864 | tf_op jit(solution)/shard_map/all_to_all | solution.py:134
  226.8 18.9 %copy-start.5 = (f32[128,1]{0,1:T(1,128)S(1)}, f32[128,1]{0,1:T(1,128)}, u32[]{:S(2)}) copy-start(f32[128,1]{0,1:T(1,128)} %param.10) | copy-start | bytes 1540
  248.7 13.2 %all-to-all-start.7 = ((bf16[8,128,256]{2,1,0:T(8,128)(2,1)}), bf16[8,128,256]{2,1,0:T(8,128)(2,1)S(1)}, u32[]{:S(2)}, u32[]{:S(2)}) async-start(bf16[8,128,256]{2,1,0:T(8,128)(2,1)} %convolution_convert_fusion.3), calls=%async_computation.7 | async-start | bytes 1048576 | tf_op jit(solution)/shard_map/all_to_all | solution.py:145
Sparse Core Ops, SparseCore 0:
  10.5 35.0 all-gather.12
  47.4 32.3 all-gather.14
  81.7 36.2 all-gather.16
  151.4 25.3 all-gather.10
  178.5 38.9 all-gather.8
where the time goes:
time: 271 us; the launch traced here: 270 us
  waiting for transfers between devices  121 us (45%)
  starting transfers between devices  37 us (14%)
  local copies, waits for them, and re-layouts  33.1 us (12%)
  matrix products  29.3 us (11%)
  blocking collectives  23.4 us (9%)
  between operations  14 us (5%)
  other arithmetic  12.4 us (5%)
    all_gather x1, waiting for transfers between devices, body(): lax.all_gather(grads_own, 'ctx', axis=0, tiled=True)  32.8 us
    all_gather x1, waiting for transfers between devices, body(): lax.all_gather(hidden_own, 'ctx', axis=0, tiled=True)  23.1 us
    unnamed x23, local copies, waits for them, and re-layouts  21 us
    all_to_all x1, waiting for transfers between devices, body(): lax.all_to_all(send_y, 'exp', split_axis=0, concat_axis=0, tiled=True)  19.3 us
    unnamed x1, blocking collectives  13.1 us
    all_to_all x1, waiting for transfers between devices, body(): lax.all_to_all(send_x, 'exp', split_axis=0, concat_axis=0, tiled=True)  12.9 us
    all_gather x1, blocking collectives, body(): all_ids = lax.all_gather(expert_ids, 'ctx', axis=0, tiled=True)  10.3 us
    all_to_all x1, waiting for transfers between devices, body(): lax.all_to_all(group_x, 'ctx', split_axis=2, concat_axis=0, tiled=True)  8.91 us
  transfers between devices with their start and end apart: 14, of which 10 were waited for; matrix products, arithmetic and copies ran while one was open for 24% of the time, Pallas kernels for 0%

commit v1 on v0

--- a/solution.py
+++ b/solution.py
@@ -2,6 +2,19 @@
 import jax.numpy as jnp
 from jax import lax
 from jax.sharding import PartitionSpec as P
+
+
+def gather_around(array, axis, dim):
+    ways = lax.axis_size(axis)
+    up = [(d, (d + 1) % ways) for d in range(ways)]
+    down = [(d, (d - 1) % ways) for d in range(ways)]
+    earlier, later = ([array], [array])
+    for _ in range(ways // 2):
+        earlier.append(lax.ppermute(earlier[-1], axis, up))
+    for _ in range((ways - 1) // 2):
+        later.append(lax.ppermute(later[-1], axis, down))
+    line = jnp.concatenate([*earlier[::-1], *later[1:]], axis=dim)
+    return jnp.roll(line, (lax.axis_index(axis) - ways // 2) * array.shape[dim], axis=dim)
 
 
 def slot_table(route_ids, expert_count, capacity):
@@ -43,7 +56,7 @@
     units = w_gate.shape[2]
     row_count = ctx_size * exp_size * capacity
     own_rows = row_count // ctx_size
-    all_ids = lax.all_gather(expert_ids, "ctx", axis=0, tiled=True)
+    all_ids = gather_around(expert_ids, "ctx", 0)
     tables = slot_table(all_ids.reshape(ctx_size, slot_count), expert_count, capacity)
     token_slots = jnp.repeat(tokens, route_count, axis=0)
     scaled = (

time: 271 us -> 285 us (1.052)
  waiting for transfers between devices: 121 us -> 133 us
  starting transfers between devices: 37 us -> 47.5 us
  blocking collectives: 23.4 us -> 13.1 us
    all_gather x1 -> x0, blocking collectives: 10.3 us -> none  [body(): all_ids = lax.all_gather(expert_ids, 'ctx', axis=0, tiled=True)]
    ppermute x0 -> x7, starting transfers between devices: none -> 8.71 us  [the longest x3 8.19 us: gather_around(): later.append(lax.ppermute(later[-1], axis, down))]
    ppermute x0 -> x7, waiting for transfers between devices: none -> 7.61 us  [the longest x4 7.53 us: gather_around(): earlier.append(lax.ppermute(earlier[-1], axis, up))]
    all_to_all x1, waiting for transfers between devices: 7.3 us -> 11.5 us  [body(): lax.all_to_all(group_y, 'ctx', split_axis=2, concat_axis=0, tiled=True)]
    unnamed x23 -> x38, local copies, waits for them, and re-layouts: 21 us -> 22.4 us
  transfers between devices with their start and end apart: 14 -> 21, of which waited for: 10 -> 15; matrix products, arithmetic and copies ran while one was open for 24% -> 23% of each run, Pallas kernels for 0% -> 0%
where the time goes in v1:
time: 285 us; the launch traced here: 284 us
  waiting for transfers between devices  133 us (47%)
  starting transfers between devices  47.5 us (17%)
  local copies, waits for them, and re-layouts  34.5 us (12%)
  matrix products  29.3 us (10%)
  between operations  14 us (5%)
  blocking collectives  13.1 us (5%)
  other arithmetic  12.4 us (4%)
    all_gather x1, waiting for transfers between devices, body(): lax.all_gather(grads_own, 'ctx', axis=0, tiled=True)  32.8 us
    all_gather x1, waiting for transfers between devices, body(): lax.all_gather(hidden_own, 'ctx', axis=0, tiled=True)  25.3 us
    unnamed x38, local copies, waits for them, and re-layouts  22.4 us
    all_to_all x1, waiting for transfers between devices, body(): lax.all_to_all(send_y, 'exp', split_axis=0, concat_axis=0, tiled=True)  16.7 us
    unnamed x1, blocking collectives  13.1 us
    all_to_all x1, waiting for transfers between devices, body(): lax.all_to_all(send_x, 'exp', split_axis=0, concat_axis=0, tiled=True)  12.3 us
    all_to_all x1, waiting for transfers between devices, body(): lax.all_to_all(group_y, 'ctx', split_axis=2, concat_axis=0, tiled=True)  11.5 us
    all_to_all x1, waiting for transfers between devices, body(): lax.all_to_all(group_x, 'ctx', split_axis=2, concat_axis=0, tiled=True)  11.3 us
  transfers between devices with their start and end apart: 21, of which 15 were waited for; matrix products, arithmetic and copies ran while one was open for 23% of the time, Pallas kernels for 0%

profile of v1, /device:TPU:0, one launch (start us, length us, event | category | flops | bytes accessed | tf_op | source)
XLA Modules:
  0.0 283.8 jit_solution(12998682724322358080)
XLA Ops:
  14.8 3.9 %collective-permute-done.1 = s32[128,1]{0,1:T(1,128)S(1)} collective-permute-done((s32[128,1]{0,1:T(1,128)S(1)}, s32[128,1]{0,1:T(1,128)S(1)}, u32[]{:S(2)}, u32[]{:S(2)}) %collective-permute-start.1) | collective-permute-done | bytes 544 | tf_op jit(solution)/shard_map/ppermute | solution.py:13
  33.0 5.6 %all-to-all-start = ((bf16[4,48,2048]{2,1,0:T(8,128)(2,1)}), bf16[4,48,2048]{2,1,0:T(8,128)(2,1)S(1)}, u32[]{:S(2)}, u32[]{:S(2)}) async-start(bf16[4,48,2048]{2,1,0:T(8,128)(2,1)} %bitcast.3), calls=%async_computation | async-start | bytes 1572864 | tf_op jit(solution)/shard_map/all_to_all | solution.py:74
  39.9 16.7 %all-to-all-done = bf16[4,48,2048]{2,1,0:T(8,128)(2,1)S(1)} async-done(((bf16[4,48,2048]{2,1,0:T(8,128)(2,1)}), bf16[4,48,2048]{2,1,0:T(8,128)(2,1)S(1)}, u32[]{:S(2)}, u32[]{:S(2)}) %all-to-all-start) | async-done | bytes 786464 | tf_op jit(solution)/shard_map/all_to_all | solution.py:74
  57.5 3.5 %all-to-all-start.3 = ((bf16[4,48,2048]{2,1,0:T(8,128)(2,1)}), bf16[4,48,2048]{2,1,0:T(8,128)(2,1)S(1)}, u32[]{:S(2)}, u32[]{:S(2)}) async-start(bf16[4,48,2048]{2,1,0:T(8,128)(2,1)} %bitcast.10), calls=%async_computation.3 | async-start | bytes 1572864 | tf_op jit(solution)/shard_map/all_to_all | solution.py:73
  63.9 4.0 %reshape.98 = bf16[8,2,24576]{2,1,0:T(2,128)(2,1)} reshape(bf16[2048,4,48]{2,1,0:T(4,128)(2,1)S(1)} %bitcast.76) | data formatting | bytes 1572864
  67.8 12.3 %all-to-all-done.3 = bf16[4,48,2048]{2,1,0:T(8,128)(2,1)S(1)} async-done(((bf16[4,48,2048]{2,1,0:T(8,128)(2,1)}), bf16[4,48,2048]{2,1,0:T(8,128)(2,1)S(1)}, u32[]{:S(2)}, u32[]{:S(2)}) %all-to-all-start.3) | async-done | bytes 786464 | tf_op jit(solution)/shard_map/all_to_all | solution.py:73
  80.1 5.3 %all-to-all-start.1 = ((bf16[8,2,24576]{2,1,0:T(2,128)(2,1)}), bf16[8,2,24576]{2,1,0:T(2,128)(2,1)}, u32[]{:S(2)}, u32[]{:S(2)}) async-start(bf16[8,2,24576]{2,1,0:T(2,128)(2,1)} %reshape.98), calls=%async_computation.1 | async-start | bytes 1572864 | tf_op jit(solution)/shard_map/all_to_all | solution.py:78
  86.7 4.0 %reshape.100 = bf16[8,2,24576]{2,1,0:T(2,128)(2,1)} reshape(bf16[2048,4,48]{2,1,0:T(4,128)(2,1)S(1)} %bitcast.77) | data formatting | bytes 1572864
  90.7 11.5 %all-to-all-done.1 = bf16[8,2,24576]{2,1,0:T(2,128)(2,1)} async-done(((bf16[8,2,24576]{2,1,0:T(2,128)(2,1)}), bf16[8,2,24576]{2,1,0:T(2,128)(2,1)}, u32[]{:S(2)}, u32[]{:S(2)}) %all-to-all-start.1) | async-done | bytes 786464 | tf_op jit(solution)/shard_map/all_to_all | solution.py:78
  102.2 3.5 %all-to-all-start.4 = ((bf16[8,2,24576]{2,1,0:T(2,128)(2,1)}), bf16[8,2,24576]{2,1,0:T(2,128)(2,1)S(1)}, u32[]{:S(2)}, u32[]{:S(2)}) async-start(bf16[8,2,24576]{2,1,0:T(2,128)(2,1)} %reshape.100), calls=%async_computation.4 | async-start | bytes 1572864 | tf_op jit(solution)/shard_map/all_to_all | solution.py:77
  105.8 5.7 %reshape.99 = bf16[2048,4,48]{2,1,0:T(4,128)(2,1)S(1)} reshape(bf16[8,2,24576]{2,1,0:T(2,128)(2,1)} %all-to-all-done.1) | data formatting | bytes 1572864
  113.6 11.3 %all-to-all-done.4 = bf16[8,2,24576]{2,1,0:T(2,128)(2,1)S(1)} async-done(((bf16[8,2,24576]{2,1,0:T(2,128)(2,1)}), bf16[8,2,24576]{2,1,0:T(2,128)(2,1)S(1)}, u32[]{:S(2)}, u32[]{:S(2)}) %all-to-all-start.4) | async-done | bytes 786464 | tf_op jit(solution)/shard_map/all_to_all | solution.py:77
  124.9 4.4 %all-to-all-start.2 = ((bf16[8,192,256]{2,1,0:T(8,128)(2,1)}), bf16[8,192,256]{2,1,0:T(8,128)(2,1)}, u32[]{:S(2)}, u32[]{:S(2)}) async-start(bf16[8,192,256]{2,1,0:T(8,128)(2,1)} %bitcast.7), calls=%async_computation.2 | async-start | bytes 1572864 | tf_op jit(solution)/shard_map/all_to_all | solution.py:101
  133.5 8.2 %all-to-all-done.2 = bf16[8,192,256]{2,1,0:T(8,128)(2,1)} async-done(((bf16[8,192,256]{2,1,0:T(8,128)(2,1)}), bf16[8,192,256]{2,1,0:T(8,128)(2,1)}, u32[]{:S(2)}, u32[]{:S(2)}) %all-to-all-start.2) | async-done | bytes 786464 | tf_op jit(solution)/shard_map/all_to_all | solution.py:101
  141.7 3.5 %all-to-all-start.5 = ((bf16[8,192,256]{2,1,0:T(8,128)(2,1)}), bf16[8,192,256]{2,1,0:T(8,128)(2,1)S(1)}, u32[]{:S(2)}, u32[]{:S(2)}) async-start(bf16[8,192,256]{2,1,0:T(8,128)(2,1)} %bitcast.13), calls=%async_computation.5 | async-start | bytes 1572864 | tf_op jit(solution)/shard_map/all_to_all | solution.py:100
  148.3 5.9 %pad_maximum_fusion = bf16[2048,1536]{1,0:T(8,128)(2,1)} fusion(bf16[2048,768]{1,0:T(8,128)(2,1)} %bitcast.83, bf16[2048,768]{1,0:T(8,128)(2,1)} %bitcast.82), kind=kLoop, calls=%fused_computation.1 | loop fusion | flops 12582912 | bytes 12582912 | tf_op jit(solution)/shard_map/concatenate | solution.py:108
  157.8 4.2 %convert_reduce_fusion = f32[192,1536]{1,0:T(8,128)S(1)} fusion(bf16[8,256,1536]{2,1,0:T(8,128)(2,1)} %bitcast.80, bf16[8,192,256]{2,1,0:T(8,128)(2,1)S(1)} %all-to-all-done.5), kind=kOutput, calls=%fused_computation | convolution fusion | flops 1214742528 | bytes 8257536 | tf_op jit(solution)/shard_map/rcd,cdf->crf/dot_general | solution.py:111
  165.5 25.3 %all-gather.11.cloned.1.call-done = bf16[1536,768]{1,0:T(8,128)(2,1)} async-done(((bf16[192,768]{1,0:T(8,128)(2,1)}), bf16[1536,768]{1,0:T(8,128)(2,1)}) %all-gather.11.cloned.1.call-update) | async-done | bytes 2359312 | tf_op jit(solution)/shard_map/all_gather | solution.py:128
  194.1 4.6 %all-to-all-start.8 = ((f32[4,1,384]{2,1,0:T(1,128)}), f32[4,1,384]{2,1,0:T(1,128)S(1)}, u32[]{:S(2)}, u32[]{:S(2)}) async-start(f32[4,1,384]{2,1,0:T(1,128)} %reshape.102), calls=%async_computation.8 | async-start | bytes 12288 | tf_op jit(solution)/shard_map/all_to_all | solution.py:148
  198.7 32.8 %all-gather.9.cloned.1.call-done = bf16[1536,1536]{1,0:T(8,128)(2,1)} async-done(((bf16[192,1536]{1,0:T(8,128)(2,1)}), bf16[1536,1536]{1,0:T(8,128)(2,1)}) %all-gather.9.cloned.1.call-update) | async-done | bytes 4718608 | tf_op jit(solution)/shard_map/all_gather | solution.py:129
  231.6 3.8 %convolution_convert_fusion = bf16[1536,256]{1,0:T(8,128)(2,1)S(1)} fusion(bf16[1536,1536]{1,0:T(8,128)(2,1)} %all-gather.9.cloned.1.call-done, bf16[256,768]{1,0:T(8,128)(2,1)S(1)} %bitcast.88, bf16[256,768]{1,0:T(8,128)(2,1)S(1)} %bitcast.87), kind=kOutput, calls=%fused_computation.4 | convolution fusion | flops 1209925632 | bytes 6291456 | tf_op jit(solution)/shard_map/dot_general | solution.py:94
  236.3 4.6 %all-to-all-start.6 = ((bf16[8,4,48,256]{3,2,0,1:T(8,128)(2,1)}), bf16[8,4,48,256]{3,2,0,1:T(8,128)(2,1)S(1)}, u32[]{:S(2)}, u32[]{:S(2)}) async-start(bf16[8,4,48,256]{3,2,0,1:T(8,128)(2,1)} %copy.93), calls=%async_computation.6 | async-start | bytes 1572864 | tf_op jit(solution)/shard_map/all_to_all | solution.py:147
  246.7 13.1 %all-reduce = f32[8,128]{1,0:T(8,128)S(1)} all-reduce(f32[8,128]{1,0:T(8,128)S(1)} %bitcast.93), channel_id=5, replica_groups=mesh['ctx'=8,'exp'=4] {'ctx'}, use_global_device_ids=true, to_apply=%region_5.6.clone | all-reduce | flops 1024 | bytes 8192
  262.8 3.5 %all-to-all-start.7 = ((bf16[8,128,256]{2,1,0:T(8,128)(2,1)}), bf16[8,128,256]{2,1,0:T(8,128)(2,1)S(1)}, u32[]{:S(2)}, u32[]{:S(2)}) async-start(bf16[8,128,256]{2,1,0:T(8,128)(2,1)} %convolution_convert_fusion.3), calls=%async_computation.7 | async-start | bytes 1048576 | tf_op jit(solution)/shard_map/all_to_all | solution.py:158
  (98 shorter events, 68.6 us)
Async XLA Ops:
  7.2 31.5 %copy-start = (bf16[128,2048]{1,0:T(8,128)(2,1)S(1)}, bf16[128,2048]{1,0:T(8,128)(2,1)}, u32[]{:S(2)}) copy-start(bf16[128,2048]{1,0:T(8,128)(2,1)} %param.7) | copy-start | bytes 1572868
  7.2 138.1 %all-gather.13.cloned.1.call-start = ((), (), s32[]{:S(2)}) async-start(), calls=%async_computation.11 | async-start | bytes 3538944 | tf_op jit(solution)/shard_map/all_gather | solution.py:106
  9.2 139.1 %all-gather.15.cloned.1.call-start = ((), (), s32[]{:S(2)}) async-start(), calls=%async_computation.12 | async-start | bytes 3538944 | tf_op jit(solution)/shard_map/all_gather | solution.py:104
  10.0 138.4 %all-gather.17.cloned.1.call-start = ((), (), s32[]{:S(2)}) async-start(), calls=%async_computation.13 | async-start | bytes 3538944 | tf_op jit(solution)/shard_map/all_gather | solution.py:105
  10.0 4.7 %collective-permute-start = (s32[128,1]{0,1:T(1,128)}, s32[128,1]{0,1:T(1,128)S(1)}, u32[]{:S(2)}, u32[]{:S(2)}) collective-permute-start(s32[128,1]{0,1:T(1,128)} %param.9), channel_id=1, source_target_pairs={{0,4},{4,8},{8,12},{12,16},{16,20},{20,24},{24,28},{28,0},{1,5},{5... | collective-permute-start | bytes 1544 | tf_op jit(solution)/shard_map/ppermute | solution.py:13
  10.5 8.1 %collective-permute-start.4 = (s32[128,1]{0,1:T(1,128)}, s32[128,1]{0,1:T(1,128)S(1)}, u32[]{:S(2)}, u32[]{:S(2)}) collective-permute-start(s32[128,1]{0,1:T(1,128)} %param.9), channel_id=1, source_target_pairs={{0,28},{4,0},{8,4},{12,8},{16,12},{20,16},{24,20},{28,24},{1,29},{... | collective-permute-start | bytes 1544 | tf_op jit(solution)/shard_map/ppermute | solution.py:15
  14.8 3.9 %collective-permute-start.1 = (s32[128,1]{0,1:T(1,128)S(1)}, s32[128,1]{0,1:T(1,128)S(1)}, u32[]{:S(2)}, u32[]{:S(2)}) collective-permute-start(s32[128,1]{0,1:T(1,128)S(1)} %collective-permute-done), channel_id=1, source_target_pairs={{0,4},{4,8},{8,12},{12,16},{16,20},{20,24},{24,28},{28,0},{1,5},{5... | collective-permute-start | bytes 1544 | tf_op jit(solution)/shard_map/ppermute | solution.py:13
  18.6 3.9 %collective-permute-start.2 = (s32[128,1]{0,1:T(1,128)S(1)}, s32[128,1]{0,1:T(1,128)S(1)}, u32[]{:S(2)}, u32[]{:S(2)}) collective-permute-start(s32[128,1]{0,1:T(1,128)S(1)} %collective-permute-done.1), channel_id=1, source_target_pairs={{0,4},{4,8},{8,12},{12,16},{16,20},{20,24},{24,28},{28,0},{1,5},{5... | collective-permute-start | bytes 1544 | tf_op jit(solution)/shard_map/ppermute | solution.py:13
  18.6 3.9 %collective-permute-start.5 = (s32[128,1]{0,1:T(1,128)S(1)}, s32[128,1]{0,1:T(1,128)S(1)}, u32[]{:S(2)}, u32[]{:S(2)}) collective-permute-start(s32[128,1]{0,1:T(1,128)S(1)} %collective-permute-done.4), channel_id=1, source_target_pairs={{0,28},{4,0},{8,4},{12,8},{16,12},{20,16},{24,20},{28,24},{1,29},{... | collective-permute-start | bytes 1544 | tf_op jit(solution)/shard_map/ppermute | solution.py:15
  22.5 3.9 %collective-permute-start.3 = (s32[128,1]{0,1:T(1,128)S(1)}, s32[128,1]{0,1:T(1,128)S(1)}, u32[]{:S(2)}, u32[]{:S(2)}) collective-permute-start(s32[128,1]{0,1:T(1,128)S(1)} %collective-permute-done.2), channel_id=1, source_target_pairs={{0,4},{4,8},{8,12},{12,16},{16,20},{20,24},{24,28},{28,0},{1,5},{5... | collective-permute-start | bytes 1544 | tf_op jit(solution)/shard_map/ppermute | solution.py:13
  22.6 4.5 %collective-permute-start.6 = (s32[128,1]{0,1:T(1,128)S(1)}, s32[128,1]{0,1:T(1,128)S(1)}, u32[]{:S(2)}, u32[]{:S(2)}) collective-permute-start(s32[128,1]{0,1:T(1,128)S(1)} %collective-permute-done.5), channel_id=1, source_target_pairs={{0,28},{4,0},{8,4},{12,8},{16,12},{20,16},{24,20},{28,24},{1,29},{... | collective-permute-start | bytes 1544 | tf_op jit(solution)/shard_map/ppermute | solution.py:15
  33.0 23.6 %all-to-all-start = ((bf16[4,48,2048]{2,1,0:T(8,128)(2,1)}), bf16[4,48,2048]{2,1,0:T(8,128)(2,1)S(1)}, u32[]{:S(2)}, u32[]{:S(2)}) async-start(bf16[4,48,2048]{2,1,0:T(8,128)(2,1)} %bitcast.3), calls=%async_computation | async-start | bytes 1572864 | tf_op jit(solution)/shard_map/all_to_all | solution.py:74
  57.5 22.6 %all-to-all-start.3 = ((bf16[4,48,2048]{2,1,0:T(8,128)(2,1)}), bf16[4,48,2048]{2,1,0:T(8,128)(2,1)S(1)}, u32[]{:S(2)}, u32[]{:S(2)}) async-start(bf16[4,48,2048]{2,1,0:T(8,128)(2,1)} %bitcast.10), calls=%async_computation.3 | async-start | bytes 1572864 | tf_op jit(solution)/shard_map/all_to_all | solution.py:73
  80.1 22.1 %all-to-all-start.1 = ((bf16[8,2,24576]{2,1,0:T(2,128)(2,1)}), bf16[8,2,24576]{2,1,0:T(2,128)(2,1)}, u32[]{:S(2)}, u32[]{:S(2)}) async-start(bf16[8,2,24576]{2,1,0:T(2,128)(2,1)} %reshape.98), calls=%async_computation.1 | async-start | bytes 1572864 | tf_op jit(solution)/shard_map/all_to_all | solution.py:78
  102.2 22.6 %all-to-all-start.4 = ((bf16[8,2,24576]{2,1,0:T(2,128)(2,1)}), bf16[8,2,24576]{2,1,0:T(2,128)(2,1)S(1)}, u32[]{:S(2)}, u32[]{:S(2)}) async-start(bf16[8,2,24576]{2,1,0:T(2,128)(2,1)} %reshape.100), calls=%async_computation.4 | async-start | bytes 1572864 | tf_op jit(solution)/shard_map/all_to_all | solution.py:77
  124.9 16.8 %all-to-all-start.2 = ((bf16[8,192,256]{2,1,0:T(8,128)(2,1)}), bf16[8,192,256]{2,1,0:T(8,128)(2,1)}, u32[]{:S(2)}, u32[]{:S(2)}) async-start(bf16[8,192,256]{2,1,0:T(8,128)(2,1)} %bitcast.7), calls=%async_computation.2 | async-start | bytes 1572864 | tf_op jit(solution)/shard_map/all_to_all | solution.py:101
  141.7 16.1 %all-to-all-start.5 = ((bf16[8,192,256]{2,1,0:T(8,128)(2,1)}), bf16[8,192,256]{2,1,0:T(8,128)(2,1)S(1)}, u32[]{:S(2)}, u32[]{:S(2)}) async-start(bf16[8,192,256]{2,1,0:T(8,128)(2,1)} %bitcast.13), calls=%async_computation.5 | async-start | bytes 1572864 | tf_op jit(solution)/shard_map/all_to_all | solution.py:100
  145.2 45.6 %all-gather.11.cloned.1.call-start = ((), (), s32[]{:S(2)}) async-start(), calls=%async_computation.10 | async-start | bytes 2654208 | tf_op jit(solution)/shard_map/all_gather | solution.py:128
  163.1 68.4 %all-gather.9.cloned.1.call-start = ((), (), s32[]{:S(2)}) async-start(), calls=%async_computation.9 | async-start | bytes 5308416 | tf_op jit(solution)/shard_map/all_gather | solution.py:129
  164.0 67.5 %copy-start.3 = (bf16[1,256,768]{2,1,0:T(8,128)(2,1)S(1)}, bf16[1,256,768]{2,1,0:T(8,128)(2,1)}, u32[]{:S(2)}) copy-start(bf16[1,256,768]{2,1,0:T(8,128)(2,1)} %param.11) | copy-start | bytes 1179652
  164.0 67.5 %copy-start.4 = (bf16[1,256,768]{2,1,0:T(8,128)(2,1)S(1)}, bf16[1,256,768]{2,1,0:T(8,128)(2,1)}, u32[]{:S(2)}) copy-start(bf16[1,256,768]{2,1,0:T(8,128)(2,1)} %param.12) | copy-start | bytes 1179652
  194.1 42.1 %all-to-all-start.8 = ((f32[4,1,384]{2,1,0:T(1,128)}), f32[4,1,384]{2,1,0:T(1,128)S(1)}, u32[]{:S(2)}, u32[]{:S(2)}) async-start(f32[4,1,384]{2,1,0:T(1,128)} %reshape.102), calls=%async_computation.8 | async-start | bytes 12288 | tf_op jit(solution)/shard_map/all_to_all | solution.py:148
  236.3 25.1 %all-to-all-start.6 = ((bf16[8,4,48,256]{3,2,0,1:T(8,128)(2,1)}), bf16[8,4,48,256]{3,2,0,1:T(8,128)(2,1)S(1)}, u32[]{:S(2)}, u32[]{:S(2)}) async-start(bf16[8,4,48,256]{3,2,0,1:T(8,128)(2,1)} %copy.93), calls=%async_computation.6 | async-start | bytes 1572864 | tf_op jit(solution)/shard_map/all_to_all | solution.py:147
  262.8 13.2 %all-to-all-start.7 = ((bf16[8,128,256]{2,1,0:T(8,128)(2,1)}), bf16[8,128,256]{2,1,0:T(8,128)(2,1)S(1)}, u32[]{:S(2)}, u32[]{:S(2)}) async-start(bf16[8,128,256]{2,1,0:T(8,128)(2,1)} %convolution_convert_fusion.3), calls=%async_computation.7 | async-start | bytes 1048576 | tf_op jit(solution)/shard_map/all_to_all | solution.py:158
  (4 other events, 54.2 us)
Sparse Core Ops, SparseCore 0:
  10.5 35.0 all-gather.12
  47.4 32.3 all-gather.14
  81.7 42.0 all-gather.16
  163.2 27.5 all-gather.10
  192.6 38.9 all-gather.8
